TPU v7x, 32 devices: a whole 2x2x4 slice. The times are simulated.
32 devices in a mesh: gx: 4 (over y, x), gy: 8 (over z, core).
Axes of the slice: x: 2, y: 2, z: 4, core: 2. Of those that a mesh axis runs over, the one named last changes fastest.
Arguments:
- probes: float32 [24, 48, 64, 128], P('gx', 'gy'), may hold values from -6 to 6
- pair_blocks: float32 [24, 48, 9, 128, 128], P('gx', 'gy'), may hold values from -0.09375 to 0.09375
- partners: int32 [24, 48, 9], P('gx', 'gy'), may hold values from 0 to 1151, as said below
- shifts: int32 [2, 24, 48, 9], P(None, 'gx', 'gy'), may hold values from -1 to 1, as said below
- counts: int32 [24, 48], P('gx', 'gy'), may hold values from 1 to 9, as said below
- kpoint: float32 [2], replicated, may hold values from -3.140625 to 3.140625
Outputs:
- last_vector: float32 [24, 48, 64, 128], P('gx', 'gy')
- intersections: float32 [3, 2, 32], replicated
Inputs may be any that keep to these rules, and one draw needn't show every extreme that they name: `partners`: slot 0 of cell (x, y) names the cell itself; slots 1 to 8 name its eight neighbouring cells (x + dx, y + dy) with dx, dy in -1..1 taken periodically modulo 24 and 48, each once, in no fixed order. shifts[0, x, y, s] = (x + dx - px) / 24 and shifts[1, x, y, s] = (y + dy - py) / 48 for the slot's offset (dx, dy) and partner cell (px, py). `counts`: slots at or beyond a cell's count are padding; some cell has all 9 slots live.
All inputs are finite; a program needn't handle non-finite values.
Results may differ from a plain program's by a relative error of at most 0.0001.
Values sent between devices are 32-bit elements; how exact they have to be, the bound alone decides.
A program may use at most 128 MiB of HBM per device.

v0:
```python
import math
import jax
import jax.numpy as jnp
from jax import lax
from jax.sharding import PartitionSpec as P

STEPS = 3


def with_halo(cells, sides, width):
    for axis, dim in sides:
        count = lax.axis_size(axis)
        head = lax.slice_in_dim(cells, 0, width, axis=dim)
        tail = lax.slice_in_dim(cells, cells.shape[dim] - width, cells.shape[dim], axis=dim)
        cells = jnp.concatenate(
            [
                lax.ppermute(tail, axis, [(i, (i + 1) % count) for i in range(count)]),
                cells,
                lax.ppermute(head, axis, [((i + 1) % count, i) for i in range(count)]),
            ],
            axis=dim,
        )
    return cells


def intersection(first, other):
    half = first.shape[2] // 2
    first_re, first_im = (first[:, :, :half], first[:, :, half:])
    other_re, other_im = (other[:, :, :half], other[:, :, half:])
    real_part = jnp.sum(first_re * other_re + first_im * other_im, axis=(0, 1, 3))
    imag_part = jnp.sum(first_re * other_im - first_im * other_re, axis=(0, 1, 3))
    return jnp.stack([real_part, imag_part])


def extend(field):
    return with_halo(field, (("gx", 0), ("gy", 1)), 1)


def shards(probes, pair_blocks, partners, shifts, counts, kpoint):
    cells_x, cells_y, width, block = probes.shape
    slot_total = pair_blocks.shape[2]
    half = width // 2
    cells = cells_x * cells_y
    total_x = cells_x * lax.axis_size("gx")
    total_y = cells_y * lax.axis_size("gy")
    start_x = lax.axis_index("gx") * cells_x
    start_y = lax.axis_index("gy") * cells_y
    partner_x = partners // total_y
    partner_y = partners % total_y
    local_x = jnp.mod(partner_x - start_x + 1, total_x)
    local_y = jnp.mod(partner_y - start_y + 1, total_y)
    flat_partner = (local_x * (cells_y + 2) + local_y).reshape(cells, slot_total)
    angle = kpoint[0] * shifts[0].astype(jnp.float32) + kpoint[1] * shifts[1].astype(jnp.float32)
    angle = angle.reshape(cells, slot_total)
    live = (jnp.arange(slot_total, dtype=jnp.int32)[None, :] < counts.reshape(cells, 1)).astype(
        jnp.float32
    )
    cosine = jnp.cos(angle) * live
    sine = jnp.sin(angle) * live
    blocks = pair_blocks.reshape(cells, slot_total, block, block)
    slot_bound = jnp.max(counts)

    def apply_hamiltonian(field):
        source = extend(field).reshape(-1, width, block)

        def accumulate(slot, sums):
            real_sum, imag_sum = sums
            piece = jnp.take(source, flat_partner[:, slot], axis=0)
            chosen = lax.dynamic_index_in_dim(blocks, slot, 1, keepdims=False)
            product = jnp.einsum("npb,nba->npa", piece, chosen, precision=lax.Precision.HIGHEST)
            cos_part = lax.dynamic_index_in_dim(cosine, slot, 1, keepdims=False)[:, None, None]
            sin_part = lax.dynamic_index_in_dim(sine, slot, 1, keepdims=False)[:, None, None]
            real_part = product[:, :half]
            imag_part = product[:, half:]
            return (
                real_sum + cos_part * real_part - sin_part * imag_part,
                imag_sum + sin_part * real_part + cos_part * imag_part,
            )

        zeros = jnp.zeros((cells, half, block), jnp.float32)
        real_sum, imag_sum = lax.fori_loop(0, slot_bound, accumulate, (zeros, zeros))
        return jnp.concatenate([real_sum, imag_sum], axis=1).reshape(field.shape)

    scale = 1.0 / math.sqrt(total_x * total_y * block)

    def reduce_one(field):
        return lax.psum(intersection(probes, field), ("gx", "gy")) * scale

    before = probes
    current = apply_hamiltonian(probes)
    partial_list = []
    partial_list.append(reduce_one(current))
    for step in range(STEPS - 1):
        following = 2.0 * apply_hamiltonian(current) - before
        before, current = (current, following)
        partial_list.append(reduce_one(current))
    found = jnp.stack(partial_list)
    return (current, found)


def solution(mesh):
    placed = (
        P("gx", "gy", None, None),
        P("gx", "gy", None, None, None),
        P("gx", "gy", None),
        P(None, "gx", "gy", None),
        P("gx", "gy"),
        P(),
    )
    return jax.shard_map(
        shards,
        mesh=mesh,
        in_specs=placed,
        out_specs=(P("gx", "gy", None, None), P()),
        check_vma=False,
    )
```

profile of v0, /device:TPU:0, one launch (start us, length us, event | category | flops | bytes accessed | tf_op | source)
XLA Modules:
  0.0 336.3 jit_solution(18082595083658992762)
XLA Ops:
  0.6 1.1 fusion.46
  1.8 3.0 collective-permute-start
  4.8 1.0 collective-permute-start.1
  5.8 1.3 fusion.47
  7.1 2.8 sine_reduce_fusion
  11.6 3.5 %collective-permute-done.1 = f32[1,6,64,128]{3,2,1,0:T(8,128)S(1)} collective-permute-done((f32[1,6,64,128]{3,2,1,0:T(8,128)S(1)}, f32[1,6,64,128]{3,2,1,0:T(8,128)S(1)}, u32[]{:S(2)}, u32[]{:S(2)}) %collective-permute-start.1) | collective-permute-done | bytes 196640 | tf_op jit(solution)/shard_map/ppermute | solution.py:19
  15.2 1.2 copy-done.21
  16.5 3.5 %collective-permute-start.3 = (f32[8,1,64,128]{3,2,1,0:T(8,128)S(1)}, f32[8,1,64,128]{3,2,1,0:T(8,128)S(1)}, u32[]{:S(2)}, u32[]{:S(2)}) collective-permute-start(f32[8,1,64,128]{3,2,1,0:T(8,128)S(1)} %get-tuple-element.273), channel_id=1, source_target_pairs={{1,0},{2,1},{3,2},{4,3},{5,4},{6,5},{7,6},{0,7},{9,8},{10,9},{11,1... | collective-permute-start | bytes 786440 | tf_op jit(solution)/shard_map/ppermute | solution.py:19
  20.4 15.5 %copy.12 = f32[6,6,9,128,128]{4,3,1,0,2:T(8,128)} copy(f32[6,6,9,128,128]{4,3,2,1,0:T(8,128)} %param.15) | data formatting | bytes 42467328 | tf_op args[1]
  36.5 1.6 pad_maximum_fusion
  38.1 0.9 broadcast.33.clone.3
  39.0 0.9 broadcast.33.clone.4
  39.9 67.6 %while.36 = (s32[]{:T(128)}, f32[36,32,128]{2,1,0:T(8,128)}, f32[36,32,128]{2,1,0:T(8,128)}, s32[]{:T(128)}, f32[36,9]{0,1:T(8,128)S(1)}, /*index=5*/s32[36,9]{0...) while((s32[]{:T(128)}, f32[36,32,128]{2,1,0:T(8,128)}, ...), condition=%wide.region_2.4_spmd, body=%wide.region_1.3_spmd.sunk | while | flops 454460640 | bytes 20059900 | solution.py:81
  41.2 4.0 %fusion.62 = f32[36,64,128]{2,1,0:T(8,128)S(1)} fusion(f32[36,9,128,128]{3,2,0,1:T(8,128)} %get-tuple-element.523, s32[]{:T(128)S(6)} %select_n.106, f32[36,64,128]{2,1,0:T(8,128)S(1)} %gather_fusion, pred[36]{0:T(512)(128)(4,1)S(1)} %get-tuple-element.457), kind=kOutput, calls=%fused_computation.3.clone.1 | convolution fusion | flops 453279744 | bytes 4718632 | tf_op jit(solution)/shard_map/while/body/npb,nba->npa/dot_general | solution.py:70
  48.7 4.0 %fusion.62 = f32[36,64,128]{2,1,0:T(8,128)S(1)} fusion(f32[36,9,128,128]{3,2,0,1:T(8,128)} %get-tuple-element.523, s32[]{:T(128)S(6)} %select_n.106, f32[36,64,128]{2,1,0:T(8,128)S(1)} %gather_fusion, pred[36]{0:T(512)(128)(4,1)S(1)} %get-tuple-element.457), kind=kOutput, calls=%fused_computation.3.clone.1 | convolution fusion | flops 453279744 | bytes 4718632 | tf_op jit(solution)/shard_map/while/body/npb,nba->npa/dot_general | solution.py:70
  56.1 4.0 %fusion.62 = f32[36,64,128]{2,1,0:T(8,128)S(1)} fusion(f32[36,9,128,128]{3,2,0,1:T(8,128)} %get-tuple-element.523, s32[]{:T(128)S(6)} %select_n.106, f32[36,64,128]{2,1,0:T(8,128)S(1)} %gather_fusion, pred[36]{0:T(512)(128)(4,1)S(1)} %get-tuple-element.457), kind=kOutput, calls=%fused_computation.3.clone.1 | convolution fusion | flops 453279744 | bytes 4718632 | tf_op jit(solution)/shard_map/while/body/npb,nba->npa/dot_general | solution.py:70
  63.5 4.0 %fusion.62 = f32[36,64,128]{2,1,0:T(8,128)S(1)} fusion(f32[36,9,128,128]{3,2,0,1:T(8,128)} %get-tuple-element.523, s32[]{:T(128)S(6)} %select_n.106, f32[36,64,128]{2,1,0:T(8,128)S(1)} %gather_fusion, pred[36]{0:T(512)(128)(4,1)S(1)} %get-tuple-element.457), kind=kOutput, calls=%fused_computation.3.clone.1 | convolution fusion | flops 453279744 | bytes 4718632 | tf_op jit(solution)/shard_map/while/body/npb,nba->npa/dot_general | solution.py:70
  71.0 4.0 %fusion.62 = f32[36,64,128]{2,1,0:T(8,128)S(1)} fusion(f32[36,9,128,128]{3,2,0,1:T(8,128)} %get-tuple-element.523, s32[]{:T(128)S(6)} %select_n.106, f32[36,64,128]{2,1,0:T(8,128)S(1)} %gather_fusion, pred[36]{0:T(512)(128)(4,1)S(1)} %get-tuple-element.457), kind=kOutput, calls=%fused_computation.3.clone.1 | convolution fusion | flops 453279744 | bytes 4718632 | tf_op jit(solution)/shard_map/while/body/npb,nba->npa/dot_general | solution.py:70
  78.4 4.0 %fusion.62 = f32[36,64,128]{2,1,0:T(8,128)S(1)} fusion(f32[36,9,128,128]{3,2,0,1:T(8,128)} %get-tuple-element.523, s32[]{:T(128)S(6)} %select_n.106, f32[36,64,128]{2,1,0:T(8,128)S(1)} %gather_fusion, pred[36]{0:T(512)(128)(4,1)S(1)} %get-tuple-element.457), kind=kOutput, calls=%fused_computation.3.clone.1 | convolution fusion | flops 453279744 | bytes 4718632 | tf_op jit(solution)/shard_map/while/body/npb,nba->npa/dot_general | solution.py:70
  85.9 4.0 %fusion.62 = f32[36,64,128]{2,1,0:T(8,128)S(1)} fusion(f32[36,9,128,128]{3,2,0,1:T(8,128)} %get-tuple-element.523, s32[]{:T(128)S(6)} %select_n.106, f32[36,64,128]{2,1,0:T(8,128)S(1)} %gather_fusion, pred[36]{0:T(512)(128)(4,1)S(1)} %get-tuple-element.457), kind=kOutput, calls=%fused_computation.3.clone.1 | convolution fusion | flops 453279744 | bytes 4718632 | tf_op jit(solution)/shard_map/while/body/npb,nba->npa/dot_general | solution.py:70
  93.3 4.0 %fusion.62 = f32[36,64,128]{2,1,0:T(8,128)S(1)} fusion(f32[36,9,128,128]{3,2,0,1:T(8,128)} %get-tuple-element.523, s32[]{:T(128)S(6)} %select_n.106, f32[36,64,128]{2,1,0:T(8,128)S(1)} %gather_fusion, pred[36]{0:T(512)(128)(4,1)S(1)} %get-tuple-element.457), kind=kOutput, calls=%fused_computation.3.clone.1 | convolution fusion | flops 453279744 | bytes 4718632 | tf_op jit(solution)/shard_map/while/body/npb,nba->npa/dot_general | solution.py:70
  100.7 4.0 %fusion.62 = f32[36,64,128]{2,1,0:T(8,128)S(1)} fusion(f32[36,9,128,128]{3,2,0,1:T(8,128)} %get-tuple-element.523, s32[]{:T(128)S(6)} %select_n.106, f32[36,64,128]{2,1,0:T(8,128)S(1)} %gather_fusion, pred[36]{0:T(512)(128)(4,1)S(1)} %get-tuple-element.457), kind=kOutput, calls=%fused_computation.3.clone.1 | convolution fusion | flops 453279744 | bytes 4718632 | tf_op jit(solution)/shard_map/while/body/npb,nba->npa/dot_general | solution.py:70
  107.5 1.2 constant_dynamic-update-slice_fusion.4
  108.8 1.5 collective-permute-start.4
  110.4 1.4 collective-permute-start.5
  111.8 5.0 %collective-permute-done.4 = f32[1,6,64,128]{3,2,1,0:T(8,128)S(1)} collective-permute-done((f32[1,6,64,128]{3,2,1,0:T(8,128)S(1)}, f32[1,6,64,128]{3,2,1,0:T(8,128)S(1)}, u32[]{:S(2)}, u32[]{:S(2)}) %collective-permute-start.4) | collective-permute-done | bytes 196640 | tf_op jit(solution)/shard_map/ppermute | solution.py:17
  116.8 1.0 collective-permute-done.5
  118.6 3.5 %collective-permute-start.7 = (f32[8,1,64,128]{3,2,1,0:T(8,128)S(1)}, f32[8,1,64,128]{3,2,1,0:T(8,128)}, u32[]{:S(2)}, u32[]{:S(2)}) collective-permute-start(f32[8,1,64,128]{3,2,1,0:T(8,128)S(1)} %get-tuple-element.271), channel_id=1, source_target_pairs={{1,0},{2,1},{3,2},{4,3},{5,4},{6,5},{7,6},{0,7},{9,8},{10,9},{11,1... | collective-permute-start | bytes 786440 | tf_op jit(solution)/shard_map/ppermute | solution.py:19
  122.1 5.8 %collective-permute-done.6 = f32[8,1,64,128]{3,2,1,0:T(8,128)S(1)} collective-permute-done((f32[8,1,64,128]{3,2,1,0:T(8,128)S(1)}, f32[8,1,64,128]{3,2,1,0:T(8,128)S(1)}, u32[]{:S(2)}, u32[]{:S(2)}) %collective-permute-start.6) | collective-permute-done | bytes 262176 | tf_op jit(solution)/shard_map/ppermute | solution.py:17
  128.6 1.3 pad_maximum_fusion.1
  130.0 0.9 broadcast.33.clone.1
  130.9 0.9 broadcast.33.clone.2
  131.7 67.6 %while.37 = (s32[]{:T(128)}, f32[36,32,128]{2,1,0:T(8,128)}, f32[36,32,128]{2,1,0:T(8,128)}, s32[]{:T(128)}, f32[36,9]{0,1:T(8,128)S(1)}, /*index=5*/s32[36,9]{0...) while((s32[]{:T(128)}, f32[36,32,128]{2,1,0:T(8,128)}, ...), condition=%wide.region_4.6_spmd, body=%wide.region_3.5_spmd.sunk | while | flops 454460640 | bytes 20059900 | solution.py:81
  133.1 4.0 %fusion.66 = f32[36,64,128]{2,1,0:T(8,128)S(1)} fusion(f32[36,9,128,128]{3,2,0,1:T(8,128)} %get-tuple-element.559, s32[]{:T(128)S(6)} %select_n.108, f32[36,64,128]{2,1,0:T(8,128)S(1)} %gather_fusion.1, pred[36]{0:T(512)(128)(4,1)S(1)} %get-tuple-element.472), kind=kOutput, calls=%fused_computation.22.clone.1 | convolution fusion | flops 453279744 | bytes 4718632 | tf_op jit(solution)/shard_map/while/body/npb,nba->npa/dot_general | solution.py:70
  140.5 4.0 %fusion.66 = f32[36,64,128]{2,1,0:T(8,128)S(1)} fusion(f32[36,9,128,128]{3,2,0,1:T(8,128)} %get-tuple-element.559, s32[]{:T(128)S(6)} %select_n.108, f32[36,64,128]{2,1,0:T(8,128)S(1)} %gather_fusion.1, pred[36]{0:T(512)(128)(4,1)S(1)} %get-tuple-element.472), kind=kOutput, calls=%fused_computation.22.clone.1 | convolution fusion | flops 453279744 | bytes 4718632 | tf_op jit(solution)/shard_map/while/body/npb,nba->npa/dot_general | solution.py:70
  148.0 4.0 %fusion.66 = f32[36,64,128]{2,1,0:T(8,128)S(1)} fusion(f32[36,9,128,128]{3,2,0,1:T(8,128)} %get-tuple-element.559, s32[]{:T(128)S(6)} %select_n.108, f32[36,64,128]{2,1,0:T(8,128)S(1)} %gather_fusion.1, pred[36]{0:T(512)(128)(4,1)S(1)} %get-tuple-element.472), kind=kOutput, calls=%fused_computation.22.clone.1 | convolution fusion | flops 453279744 | bytes 4718632 | tf_op jit(solution)/shard_map/while/body/npb,nba->npa/dot_general | solution.py:70
  155.4 4.0 %fusion.66 = f32[36,64,128]{2,1,0:T(8,128)S(1)} fusion(f32[36,9,128,128]{3,2,0,1:T(8,128)} %get-tuple-element.559, s32[]{:T(128)S(6)} %select_n.108, f32[36,64,128]{2,1,0:T(8,128)S(1)} %gather_fusion.1, pred[36]{0:T(512)(128)(4,1)S(1)} %get-tuple-element.472), kind=kOutput, calls=%fused_computation.22.clone.1 | convolution fusion | flops 453279744 | bytes 4718632 | tf_op jit(solution)/shard_map/while/body/npb,nba->npa/dot_general | solution.py:70
  162.8 4.0 %fusion.66 = f32[36,64,128]{2,1,0:T(8,128)S(1)} fusion(f32[36,9,128,128]{3,2,0,1:T(8,128)} %get-tuple-element.559, s32[]{:T(128)S(6)} %select_n.108, f32[36,64,128]{2,1,0:T(8,128)S(1)} %gather_fusion.1, pred[36]{0:T(512)(128)(4,1)S(1)} %get-tuple-element.472), kind=kOutput, calls=%fused_computation.22.clone.1 | convolution fusion | flops 453279744 | bytes 4718632 | tf_op jit(solution)/shard_map/while/body/npb,nba->npa/dot_general | solution.py:70
  170.3 4.0 %fusion.66 = f32[36,64,128]{2,1,0:T(8,128)S(1)} fusion(f32[36,9,128,128]{3,2,0,1:T(8,128)} %get-tuple-element.559, s32[]{:T(128)S(6)} %select_n.108, f32[36,64,128]{2,1,0:T(8,128)S(1)} %gather_fusion.1, pred[36]{0:T(512)(128)(4,1)S(1)} %get-tuple-element.472), kind=kOutput, calls=%fused_computation.22.clone.1 | convolution fusion | flops 453279744 | bytes 4718632 | tf_op jit(solution)/shard_map/while/body/npb,nba->npa/dot_general | solution.py:70
  177.7 4.0 %fusion.66 = f32[36,64,128]{2,1,0:T(8,128)S(1)} fusion(f32[36,9,128,128]{3,2,0,1:T(8,128)} %get-tuple-element.559, s32[]{:T(128)S(6)} %select_n.108, f32[36,64,128]{2,1,0:T(8,128)S(1)} %gather_fusion.1, pred[36]{0:T(512)(128)(4,1)S(1)} %get-tuple-element.472), kind=kOutput, calls=%fused_computation.22.clone.1 | convolution fusion | flops 453279744 | bytes 4718632 | tf_op jit(solution)/shard_map/while/body/npb,nba->npa/dot_general | solution.py:70
  185.2 4.0 %fusion.66 = f32[36,64,128]{2,1,0:T(8,128)S(1)} fusion(f32[36,9,128,128]{3,2,0,1:T(8,128)} %get-tuple-element.559, s32[]{:T(128)S(6)} %select_n.108, f32[36,64,128]{2,1,0:T(8,128)S(1)} %gather_fusion.1, pred[36]{0:T(512)(128)(4,1)S(1)} %get-tuple-element.472), kind=kOutput, calls=%fused_computation.22.clone.1 | convolution fusion | flops 453279744 | bytes 4718632 | tf_op jit(solution)/shard_map/while/body/npb,nba->npa/dot_general | solution.py:70
  192.6 4.0 %fusion.66 = f32[36,64,128]{2,1,0:T(8,128)S(1)} fusion(f32[36,9,128,128]{3,2,0,1:T(8,128)} %get-tuple-element.559, s32[]{:T(128)S(6)} %select_n.108, f32[36,64,128]{2,1,0:T(8,128)S(1)} %gather_fusion.1, pred[36]{0:T(512)(128)(4,1)S(1)} %get-tuple-element.472), kind=kOutput, calls=%fused_computation.22.clone.1 | convolution fusion | flops 453279744 | bytes 4718632 | tf_op jit(solution)/shard_map/while/body/npb,nba->npa/dot_general | solution.py:70
  199.4 1.4 maximum_multiply_fusion
  201.3 2.9 collective-permute-start.9
  204.2 5.7 %collective-permute-done.8 = f32[1,6,64,128]{3,2,1,0:T(8,128)S(1)} collective-permute-done((f32[1,6,64,128]{3,2,1,0:T(8,128)S(1)}, f32[1,6,64,128]{3,2,1,0:T(8,128)S(1)}, u32[]{:S(2)}, u32[]{:S(2)}) %collective-permute-start.8) | collective-permute-done | bytes 196640 | tf_op jit(solution)/shard_map/ppermute | solution.py:17
  211.3 3.5 %collective-permute-start.11 = (f32[8,1,64,128]{3,2,1,0:T(8,128)S(1)}, f32[8,1,64,128]{3,2,1,0:T(8,128)}, u32[]{:S(2)}, u32[]{:S(2)}) collective-permute-start(f32[8,1,64,128]{3,2,1,0:T(8,128)S(1)} %get-tuple-element.269), channel_id=1, source_target_pairs={{1,0},{2,1},{3,2},{4,3},{5,4},{6,5},{7,6},{0,7},{9,8},{10,9},{11,1... | collective-permute-start | bytes 786440 | tf_op jit(solution)/shard_map/ppermute | solution.py:19
  214.8 5.2 %collective-permute-done.10 = f32[8,1,64,128]{3,2,1,0:T(8,128)S(1)} collective-permute-done((f32[8,1,64,128]{3,2,1,0:T(8,128)S(1)}, f32[8,1,64,128]{3,2,1,0:T(8,128)S(1)}, u32[]{:S(2)}, u32[]{:S(2)}) %collective-permute-start.10) | collective-permute-done | bytes 262176 | tf_op jit(solution)/shard_map/ppermute | solution.py:17
  220.7 1.3 pad_maximum_fusion.2
  222.0 0.9 broadcast.33
  222.9 0.9 broadcast.33.clone
  223.8 68.2 %while.38 = (s32[]{:T(128)}, f32[36,32,128]{2,1,0:T(8,128)}, f32[36,32,128]{2,1,0:T(8,128)}, s32[]{:T(128)}, f32[36,9]{0,1:T(8,128)S(1)}, /*index=5*/s32[36,9]{0...) while((s32[]{:T(128)}, f32[36,32,128]{2,1,0:T(8,128)}, ...), condition=%wide.region_6.8_spmd, body=%wide.region_5.7_spmd.sunk | while | flops 454460640 | bytes 20059900 | solution.py:81
  225.3 4.0 %fusion.70 = f32[36,64,128]{2,1,0:T(8,128)S(1)} fusion(f32[36,9,128,128]{3,2,0,1:T(8,128)} %get-tuple-element.595, s32[]{:T(128)S(6)} %select_n.110, f32[36,64,128]{2,1,0:T(8,128)S(1)} %gather_fusion.2, pred[36]{0:T(512)(128)(4,1)S(1)} %get-tuple-element.487), kind=kOutput, calls=%fused_computation.41.clone.1 | convolution fusion | flops 453279744 | bytes 4718632 | tf_op jit(solution)/shard_map/while/body/npb,nba->npa/dot_general | solution.py:70
  232.8 4.0 %fusion.70 = f32[36,64,128]{2,1,0:T(8,128)S(1)} fusion(f32[36,9,128,128]{3,2,0,1:T(8,128)} %get-tuple-element.595, s32[]{:T(128)S(6)} %select_n.110, f32[36,64,128]{2,1,0:T(8,128)S(1)} %gather_fusion.2, pred[36]{0:T(512)(128)(4,1)S(1)} %get-tuple-element.487), kind=kOutput, calls=%fused_computation.41.clone.1 | convolution fusion | flops 453279744 | bytes 4718632 | tf_op jit(solution)/shard_map/while/body/npb,nba->npa/dot_general | solution.py:70
  240.3 4.0 %fusion.70 = f32[36,64,128]{2,1,0:T(8,128)S(1)} fusion(f32[36,9,128,128]{3,2,0,1:T(8,128)} %get-tuple-element.595, s32[]{:T(128)S(6)} %select_n.110, f32[36,64,128]{2,1,0:T(8,128)S(1)} %gather_fusion.2, pred[36]{0:T(512)(128)(4,1)S(1)} %get-tuple-element.487), kind=kOutput, calls=%fused_computation.41.clone.1 | convolution fusion | flops 453279744 | bytes 4718632 | tf_op jit(solution)/shard_map/while/body/npb,nba->npa/dot_general | solution.py:70
  247.8 4.0 %fusion.70 = f32[36,64,128]{2,1,0:T(8,128)S(1)} fusion(f32[36,9,128,128]{3,2,0,1:T(8,128)} %get-tuple-element.595, s32[]{:T(128)S(6)} %select_n.110, f32[36,64,128]{2,1,0:T(8,128)S(1)} %gather_fusion.2, pred[36]{0:T(512)(128)(4,1)S(1)} %get-tuple-element.487), kind=kOutput, calls=%fused_computation.41.clone.1 | convolution fusion | flops 453279744 | bytes 4718632 | tf_op jit(solution)/shard_map/while/body/npb,nba->npa/dot_general | solution.py:70
  255.3 4.0 %fusion.70 = f32[36,64,128]{2,1,0:T(8,128)S(1)} fusion(f32[36,9,128,128]{3,2,0,1:T(8,128)} %get-tuple-element.595, s32[]{:T(128)S(6)} %select_n.110, f32[36,64,128]{2,1,0:T(8,128)S(1)} %gather_fusion.2, pred[36]{0:T(512)(128)(4,1)S(1)} %get-tuple-element.487), kind=kOutput, calls=%fused_computation.41.clone.1 | convolution fusion | flops 453279744 | bytes 4718632 | tf_op jit(solution)/shard_map/while/body/npb,nba->npa/dot_general | solution.py:70
  262.8 4.0 %fusion.70 = f32[36,64,128]{2,1,0:T(8,128)S(1)} fusion(f32[36,9,128,128]{3,2,0,1:T(8,128)} %get-tuple-element.595, s32[]{:T(128)S(6)} %select_n.110, f32[36,64,128]{2,1,0:T(8,128)S(1)} %gather_fusion.2, pred[36]{0:T(512)(128)(4,1)S(1)} %get-tuple-element.487), kind=kOutput, calls=%fused_computation.41.clone.1 | convolution fusion | flops 453279744 | bytes 4718632 | tf_op jit(solution)/shard_map/while/body/npb,nba->npa/dot_general | solution.py:70
  270.3 4.0 %fusion.70 = f32[36,64,128]{2,1,0:T(8,128)S(1)} fusion(f32[36,9,128,128]{3,2,0,1:T(8,128)} %get-tuple-element.595, s32[]{:T(128)S(6)} %select_n.110, f32[36,64,128]{2,1,0:T(8,128)S(1)} %gather_fusion.2, pred[36]{0:T(512)(128)(4,1)S(1)} %get-tuple-element.487), kind=kOutput, calls=%fused_computation.41.clone.1 | convolution fusion | flops 453279744 | bytes 4718632 | tf_op jit(solution)/shard_map/while/body/npb,nba->npa/dot_general | solution.py:70
  277.7 4.0 %fusion.70 = f32[36,64,128]{2,1,0:T(8,128)S(1)} fusion(f32[36,9,128,128]{3,2,0,1:T(8,128)} %get-tuple-element.595, s32[]{:T(128)S(6)} %select_n.110, f32[36,64,128]{2,1,0:T(8,128)S(1)} %gather_fusion.2, pred[36]{0:T(512)(128)(4,1)S(1)} %get-tuple-element.487), kind=kOutput, calls=%fused_computation.41.clone.1 | convolution fusion | flops 453279744 | bytes 4718632 | tf_op jit(solution)/shard_map/while/body/npb,nba->npa/dot_general | solution.py:70
  285.2 4.0 %fusion.70 = f32[36,64,128]{2,1,0:T(8,128)S(1)} fusion(f32[36,9,128,128]{3,2,0,1:T(8,128)} %get-tuple-element.595, s32[]{:T(128)S(6)} %select_n.110, f32[36,64,128]{2,1,0:T(8,128)S(1)} %gather_fusion.2, pred[36]{0:T(512)(128)(4,1)S(1)} %get-tuple-element.487), kind=kOutput, calls=%fused_computation.41.clone.1 | convolution fusion | flops 453279744 | bytes 4718632 | tf_op jit(solution)/shard_map/while/body/npb,nba->npa/dot_general | solution.py:70
  292.0 1.4 maximum_multiply_fusion.1
  293.8 1.1 copy-done.16
  295.3 1.2 add_reduce_fusion.2
  296.5 39.2 %all-reduce = (f32[2,32]{1,0:T(2,128)S(1)}, f32[2,32]{1,0:T(2,128)S(1)}, f32[2,32]{1,0:T(2,128)S(1)}) all-reduce(f32[2,32]{1,0:T(2,128)S(1)} %pad_maximum_fusion.12, f32[2,32]{1,0:T(2,128)S(1)} %pad_maximum_fusion.11, f32[2,32]{1,0:T(2,128)S(1)} %pad_maximum_fusion.10), channel_id=1, replica_groups=mesh['gx'=4,'gy'=8] {'gx','gy'}, use_global_device_ids=true, to_apply=%region_15.17 | all-reduce | flops 192 | bytes 1536 | tf_op jit(solution)/shard_map/psum | solution.py:87
  (418 shorter events, 81.6 us)
Async XLA Ops:
  0.6 10.9 %copy-start.17 = (f32[6,6,64,128]{3,2,1,0:T(8,128)S(1)}, f32[6,6,64,128]{3,2,1,0:T(8,128)}, u32[]{:S(2)}) copy-start(f32[6,6,64,128]{3,2,1,0:T(8,128)} %param.14) | copy-start | bytes 3538948
  1.8 9.7 %collective-permute-start = (f32[1,6,64,128]{3,2,1,0:T(8,128)S(1)}, f32[1,6,64,128]{3,2,1,0:T(8,128)S(1)}, u32[]{:S(2)}, u32[]{:S(2)}) collective-permute-start(f32[1,6,64,128]{3,2,1,0:T(8,128)S(1)} %get-tuple-element.281), channel_id=1, source_target_pairs={{0,8},{8,16},{16,24},{24,0},{1,9},{9,17},{17,25},{25,1},{2,10},{10... | collective-permute-start | bytes 589832 | tf_op jit(solution)/shard_map/ppermute | solution.py:17
  4.8 10.3 %collective-permute-start.1 = (f32[1,6,64,128]{3,2,1,0:T(8,128)S(1)}, f32[1,6,64,128]{3,2,1,0:T(8,128)S(1)}, u32[]{:S(2)}, u32[]{:S(2)}) collective-permute-start(f32[1,6,64,128]{3,2,1,0:T(8,128)S(1)} %get-tuple-element.280), channel_id=1, source_target_pairs={{8,0},{16,8},{24,16},{0,24},{9,1},{17,9},{25,17},{1,25},{10,2},{18... | collective-permute-start | bytes 589832 | tf_op jit(solution)/shard_map/ppermute | solution.py:19
  11.6 8.6 %copy-start.26 = (s32[6,6,9]{2,1,0:T(8,128)S(1)}, s32[6,6,9]{2,1,0:T(8,128)}, u32[]{:S(2)}) copy-start(s32[6,6,9]{2,1,0:T(8,128)} %param.16) | copy-start | bytes 3892
  16.4 20.1 %collective-permute-start.2 = (f32[8,1,64,128]{3,2,1,0:T(8,128)S(1)}, f32[8,1,64,128]{3,2,1,0:T(8,128)S(1)}, u32[]{:S(2)}, u32[]{:S(2)}) collective-permute-start(f32[8,1,64,128]{3,2,1,0:T(8,128)S(1)} %get-tuple-element.272), channel_id=1, source_target_pairs={{0,1},{1,2},{2,3},{3,4},{4,5},{5,6},{6,7},{7,0},{8,9},{9,10},{10,1... | collective-permute-start | bytes 786440 | tf_op jit(solution)/shard_map/ppermute | solution.py:17
  16.5 20.1 %collective-permute-start.3 = (f32[8,1,64,128]{3,2,1,0:T(8,128)S(1)}, f32[8,1,64,128]{3,2,1,0:T(8,128)S(1)}, u32[]{:S(2)}, u32[]{:S(2)}) collective-permute-start(f32[8,1,64,128]{3,2,1,0:T(8,128)S(1)} %get-tuple-element.273), channel_id=1, source_target_pairs={{1,0},{2,1},{3,2},{4,3},{5,4},{6,5},{7,6},{0,7},{9,8},{10,9},{11,1... | collective-permute-start | bytes 786440 | tf_op jit(solution)/shard_map/ppermute | solution.py:19
  20.4 15.5 %copy-start.27 = (s32[6,6]{1,0:T(8,128)S(1)}, s32[6,6]{1,0:T(8,128)}, u32[]{:S(2)}) copy-start(s32[6,6]{1,0:T(8,128)} %param.18) | copy-start | bytes 436
  41.2 4.1 %copy-start.4 = (f32[36,32,128]{2,1,0:T(8,128)S(1)}, f32[36,32,128]{2,1,0:T(8,128)}, u32[]{:S(2)}) copy-start(f32[36,32,128]{2,1,0:T(8,128)} %get-tuple-element.505) | copy-start | bytes 1769476 | tf_op jit(solution)/shard_map/while
  41.2 4.1 %copy-start.6 = (f32[36,32,128]{2,1,0:T(8,128)S(1)}, f32[36,32,128]{2,1,0:T(8,128)}, u32[]{:S(2)}) copy-start(f32[36,32,128]{2,1,0:T(8,128)} %get-tuple-element.506) | copy-start | bytes 1769476 | tf_op jit(solution)/shard_map/while
  48.6 4.1 %copy-start.4 = (f32[36,32,128]{2,1,0:T(8,128)S(1)}, f32[36,32,128]{2,1,0:T(8,128)}, u32[]{:S(2)}) copy-start(f32[36,32,128]{2,1,0:T(8,128)} %get-tuple-element.505) | copy-start | bytes 1769476 | tf_op jit(solution)/shard_map/while
  48.6 4.1 %copy-start.6 = (f32[36,32,128]{2,1,0:T(8,128)S(1)}, f32[36,32,128]{2,1,0:T(8,128)}, u32[]{:S(2)}) copy-start(f32[36,32,128]{2,1,0:T(8,128)} %get-tuple-element.506) | copy-start | bytes 1769476 | tf_op jit(solution)/shard_map/while
  56.1 4.1 %copy-start.4 = (f32[36,32,128]{2,1,0:T(8,128)S(1)}, f32[36,32,128]{2,1,0:T(8,128)}, u32[]{:S(2)}) copy-start(f32[36,32,128]{2,1,0:T(8,128)} %get-tuple-element.505) | copy-start | bytes 1769476 | tf_op jit(solution)/shard_map/while
  56.1 4.1 %copy-start.6 = (f32[36,32,128]{2,1,0:T(8,128)S(1)}, f32[36,32,128]{2,1,0:T(8,128)}, u32[]{:S(2)}) copy-start(f32[36,32,128]{2,1,0:T(8,128)} %get-tuple-element.506) | copy-start | bytes 1769476 | tf_op jit(solution)/shard_map/while
  63.5 4.1 %copy-start.4 = (f32[36,32,128]{2,1,0:T(8,128)S(1)}, f32[36,32,128]{2,1,0:T(8,128)}, u32[]{:S(2)}) copy-start(f32[36,32,128]{2,1,0:T(8,128)} %get-tuple-element.505) | copy-start | bytes 1769476 | tf_op jit(solution)/shard_map/while
  63.5 4.1 %copy-start.6 = (f32[36,32,128]{2,1,0:T(8,128)S(1)}, f32[36,32,128]{2,1,0:T(8,128)}, u32[]{:S(2)}) copy-start(f32[36,32,128]{2,1,0:T(8,128)} %get-tuple-element.506) | copy-start | bytes 1769476 | tf_op jit(solution)/shard_map/while
  71.0 4.1 %copy-start.4 = (f32[36,32,128]{2,1,0:T(8,128)S(1)}, f32[36,32,128]{2,1,0:T(8,128)}, u32[]{:S(2)}) copy-start(f32[36,32,128]{2,1,0:T(8,128)} %get-tuple-element.505) | copy-start | bytes 1769476 | tf_op jit(solution)/shard_map/while
  71.0 4.1 %copy-start.6 = (f32[36,32,128]{2,1,0:T(8,128)S(1)}, f32[36,32,128]{2,1,0:T(8,128)}, u32[]{:S(2)}) copy-start(f32[36,32,128]{2,1,0:T(8,128)} %get-tuple-element.506) | copy-start | bytes 1769476 | tf_op jit(solution)/shard_map/while
  78.4 4.1 %copy-start.4 = (f32[36,32,128]{2,1,0:T(8,128)S(1)}, f32[36,32,128]{2,1,0:T(8,128)}, u32[]{:S(2)}) copy-start(f32[36,32,128]{2,1,0:T(8,128)} %get-tuple-element.505) | copy-start | bytes 1769476 | tf_op jit(solution)/shard_map/while
  78.4 4.1 %copy-start.6 = (f32[36,32,128]{2,1,0:T(8,128)S(1)}, f32[36,32,128]{2,1,0:T(8,128)}, u32[]{:S(2)}) copy-start(f32[36,32,128]{2,1,0:T(8,128)} %get-tuple-element.506) | copy-start | bytes 1769476 | tf_op jit(solution)/shard_map/while
  85.8 4.1 %copy-start.4 = (f32[36,32,128]{2,1,0:T(8,128)S(1)}, f32[36,32,128]{2,1,0:T(8,128)}, u32[]{:S(2)}) copy-start(f32[36,32,128]{2,1,0:T(8,128)} %get-tuple-element.505) | copy-start | bytes 1769476 | tf_op jit(solution)/shard_map/while
  85.8 4.1 %copy-start.6 = (f32[36,32,128]{2,1,0:T(8,128)S(1)}, f32[36,32,128]{2,1,0:T(8,128)}, u32[]{:S(2)}) copy-start(f32[36,32,128]{2,1,0:T(8,128)} %get-tuple-element.506) | copy-start | bytes 1769476 | tf_op jit(solution)/shard_map/while
  93.3 4.1 %copy-start.4 = (f32[36,32,128]{2,1,0:T(8,128)S(1)}, f32[36,32,128]{2,1,0:T(8,128)}, u32[]{:S(2)}) copy-start(f32[36,32,128]{2,1,0:T(8,128)} %get-tuple-element.505) | copy-start | bytes 1769476 | tf_op jit(solution)/shard_map/while
  93.3 4.1 %copy-start.6 = (f32[36,32,128]{2,1,0:T(8,128)S(1)}, f32[36,32,128]{2,1,0:T(8,128)}, u32[]{:S(2)}) copy-start(f32[36,32,128]{2,1,0:T(8,128)} %get-tuple-element.506) | copy-start | bytes 1769476 | tf_op jit(solution)/shard_map/while
  100.7 4.1 %copy-start.4 = (f32[36,32,128]{2,1,0:T(8,128)S(1)}, f32[36,32,128]{2,1,0:T(8,128)}, u32[]{:S(2)}) copy-start(f32[36,32,128]{2,1,0:T(8,128)} %get-tuple-element.505) | copy-start | bytes 1769476 | tf_op jit(solution)/shard_map/while
  100.7 4.1 %copy-start.6 = (f32[36,32,128]{2,1,0:T(8,128)S(1)}, f32[36,32,128]{2,1,0:T(8,128)}, u32[]{:S(2)}) copy-start(f32[36,32,128]{2,1,0:T(8,128)} %get-tuple-element.506) | copy-start | bytes 1769476 | tf_op jit(solution)/shard_map/while
  108.8 19.9 %copy-start.13 = (f32[36,64,128]{2,1,0:T(8,128)}, f32[36,64,128]{2,1,0:T(8,128)S(1)}, u32[]{:S(2)}) copy-start(f32[36,64,128]{2,1,0:T(8,128)S(1)} %constant_dynamic-update-slice_fusion.3) | copy-start | bytes 3538948
  108.8 8.0 %collective-permute-start.4 = (f32[1,6,64,128]{3,2,1,0:T(8,128)S(1)}, f32[1,6,64,128]{3,2,1,0:T(8,128)S(1)}, u32[]{:S(2)}, u32[]{:S(2)}) collective-permute-start(f32[1,6,64,128]{3,2,1,0:T(8,128)S(1)} %get-tuple-element.278), channel_id=1, source_target_pairs={{0,8},{8,16},{16,24},{24,0},{1,9},{9,17},{17,25},{25,1},{2,10},{10... | collective-permute-start | bytes 589832 | tf_op jit(solution)/shard_map/ppermute | solution.py:17
  110.4 7.4 %collective-permute-start.5 = (f32[1,6,64,128]{3,2,1,0:T(8,128)S(1)}, f32[1,6,64,128]{3,2,1,0:T(8,128)S(1)}, u32[]{:S(2)}, u32[]{:S(2)}) collective-permute-start(f32[1,6,64,128]{3,2,1,0:T(8,128)S(1)} %get-tuple-element.279), channel_id=1, source_target_pairs={{8,0},{16,8},{24,16},{0,24},{9,1},{17,9},{25,17},{1,25},{10,2},{18... | collective-permute-start | bytes 589832 | tf_op jit(solution)/shard_map/ppermute | solution.py:19
  118.5 9.4 %collective-permute-start.6 = (f32[8,1,64,128]{3,2,1,0:T(8,128)S(1)}, f32[8,1,64,128]{3,2,1,0:T(8,128)S(1)}, u32[]{:S(2)}, u32[]{:S(2)}) collective-permute-start(f32[8,1,64,128]{3,2,1,0:T(8,128)S(1)} %get-tuple-element.270), channel_id=1, source_target_pairs={{0,1},{1,2},{2,3},{3,4},{4,5},{5,6},{6,7},{7,0},{8,9},{9,10},{10,1... | collective-permute-start | bytes 786440 | tf_op jit(solution)/shard_map/ppermute | solution.py:17
  118.6 10.0 %collective-permute-start.7 = (f32[8,1,64,128]{3,2,1,0:T(8,128)S(1)}, f32[8,1,64,128]{3,2,1,0:T(8,128)}, u32[]{:S(2)}, u32[]{:S(2)}) collective-permute-start(f32[8,1,64,128]{3,2,1,0:T(8,128)S(1)} %get-tuple-element.271), channel_id=1, source_target_pairs={{1,0},{2,1},{3,2},{4,3},{5,4},{6,5},{7,6},{0,7},{9,8},{10,9},{11,1... | collective-permute-start | bytes 786440 | tf_op jit(solution)/shard_map/ppermute | solution.py:19
  133.1 4.1 %copy-start.9 = (f32[36,32,128]{2,1,0:T(8,128)S(1)}, f32[36,32,128]{2,1,0:T(8,128)}, u32[]{:S(2)}) copy-start(f32[36,32,128]{2,1,0:T(8,128)} %get-tuple-element.541) | copy-start | bytes 1769476 | tf_op jit(solution)/shard_map/while
  133.1 4.1 %copy-start.11 = (f32[36,32,128]{2,1,0:T(8,128)S(1)}, f32[36,32,128]{2,1,0:T(8,128)}, u32[]{:S(2)}) copy-start(f32[36,32,128]{2,1,0:T(8,128)} %get-tuple-element.542) | copy-start | bytes 1769476 | tf_op jit(solution)/shard_map/while
  140.5 4.1 %copy-start.9 = (f32[36,32,128]{2,1,0:T(8,128)S(1)}, f32[36,32,128]{2,1,0:T(8,128)}, u32[]{:S(2)}) copy-start(f32[36,32,128]{2,1,0:T(8,128)} %get-tuple-element.541) | copy-start | bytes 1769476 | tf_op jit(solution)/shard_map/while
  140.5 4.1 %copy-start.11 = (f32[36,32,128]{2,1,0:T(8,128)S(1)}, f32[36,32,128]{2,1,0:T(8,128)}, u32[]{:S(2)}) copy-start(f32[36,32,128]{2,1,0:T(8,128)} %get-tuple-element.542) | copy-start | bytes 1769476 | tf_op jit(solution)/shard_map/while
  147.9 4.1 %copy-start.9 = (f32[36,32,128]{2,1,0:T(8,128)S(1)}, f32[36,32,128]{2,1,0:T(8,128)}, u32[]{:S(2)}) copy-start(f32[36,32,128]{2,1,0:T(8,128)} %get-tuple-element.541) | copy-start | bytes 1769476 | tf_op jit(solution)/shard_map/while
  148.0 4.1 %copy-start.11 = (f32[36,32,128]{2,1,0:T(8,128)S(1)}, f32[36,32,128]{2,1,0:T(8,128)}, u32[]{:S(2)}) copy-start(f32[36,32,128]{2,1,0:T(8,128)} %get-tuple-element.542) | copy-start | bytes 1769476 | tf_op jit(solution)/shard_map/while
  155.4 4.1 %copy-start.9 = (f32[36,32,128]{2,1,0:T(8,128)S(1)}, f32[36,32,128]{2,1,0:T(8,128)}, u32[]{:S(2)}) copy-start(f32[36,32,128]{2,1,0:T(8,128)} %get-tuple-element.541) | copy-start | bytes 1769476 | tf_op jit(solution)/shard_map/while
  155.4 4.1 %copy-start.11 = (f32[36,32,128]{2,1,0:T(8,128)S(1)}, f32[36,32,128]{2,1,0:T(8,128)}, u32[]{:S(2)}) copy-start(f32[36,32,128]{2,1,0:T(8,128)} %get-tuple-element.542) | copy-start | bytes 1769476 | tf_op jit(solution)/shard_map/while
  162.8 4.1 %copy-start.9 = (f32[36,32,128]{2,1,0:T(8,128)S(1)}, f32[36,32,128]{2,1,0:T(8,128)}, u32[]{:S(2)}) copy-start(f32[36,32,128]{2,1,0:T(8,128)} %get-tuple-element.541) | copy-start | bytes 1769476 | tf_op jit(solution)/shard_map/while
  162.8 4.1 %copy-start.11 = (f32[36,32,128]{2,1,0:T(8,128)S(1)}, f32[36,32,128]{2,1,0:T(8,128)}, u32[]{:S(2)}) copy-start(f32[36,32,128]{2,1,0:T(8,128)} %get-tuple-element.542) | copy-start | bytes 1769476 | tf_op jit(solution)/shard_map/while
  170.3 4.1 %copy-start.9 = (f32[36,32,128]{2,1,0:T(8,128)S(1)}, f32[36,32,128]{2,1,0:T(8,128)}, u32[]{:S(2)}) copy-start(f32[36,32,128]{2,1,0:T(8,128)} %get-tuple-element.541) | copy-start | bytes 1769476 | tf_op jit(solution)/shard_map/while
  170.3 4.1 %copy-start.11 = (f32[36,32,128]{2,1,0:T(8,128)S(1)}, f32[36,32,128]{2,1,0:T(8,128)}, u32[]{:S(2)}) copy-start(f32[36,32,128]{2,1,0:T(8,128)} %get-tuple-element.542) | copy-start | bytes 1769476 | tf_op jit(solution)/shard_map/while
  177.7 4.1 %copy-start.9 = (f32[36,32,128]{2,1,0:T(8,128)S(1)}, f32[36,32,128]{2,1,0:T(8,128)}, u32[]{:S(2)}) copy-start(f32[36,32,128]{2,1,0:T(8,128)} %get-tuple-element.541) | copy-start | bytes 1769476 | tf_op jit(solution)/shard_map/while
  177.7 4.1 %copy-start.11 = (f32[36,32,128]{2,1,0:T(8,128)S(1)}, f32[36,32,128]{2,1,0:T(8,128)}, u32[]{:S(2)}) copy-start(f32[36,32,128]{2,1,0:T(8,128)} %get-tuple-element.542) | copy-start | bytes 1769476 | tf_op jit(solution)/shard_map/while
  185.1 4.1 %copy-start.9 = (f32[36,32,128]{2,1,0:T(8,128)S(1)}, f32[36,32,128]{2,1,0:T(8,128)}, u32[]{:S(2)}) copy-start(f32[36,32,128]{2,1,0:T(8,128)} %get-tuple-element.541) | copy-start | bytes 1769476 | tf_op jit(solution)/shard_map/while
  192.6 4.1 %copy-start.9 = (f32[36,32,128]{2,1,0:T(8,128)S(1)}, f32[36,32,128]{2,1,0:T(8,128)}, u32[]{:S(2)}) copy-start(f32[36,32,128]{2,1,0:T(8,128)} %get-tuple-element.541) | copy-start | bytes 1769476 | tf_op jit(solution)/shard_map/while
  192.6 4.1 %copy-start.11 = (f32[36,32,128]{2,1,0:T(8,128)S(1)}, f32[36,32,128]{2,1,0:T(8,128)}, u32[]{:S(2)}) copy-start(f32[36,32,128]{2,1,0:T(8,128)} %get-tuple-element.542) | copy-start | bytes 1769476 | tf_op jit(solution)/shard_map/while
  201.1 19.5 %copy-start.15 = (f32[6,6,64,128]{3,2,1,0:T(8,128)}, f32[6,6,64,128]{3,2,1,0:T(8,128)S(1)}, u32[]{:S(2)}) copy-start(f32[6,6,64,128]{3,2,1,0:T(8,128)S(1)} %sub.47) | copy-start | bytes 3538948
  201.2 8.7 %collective-permute-start.8 = (f32[1,6,64,128]{3,2,1,0:T(8,128)S(1)}, f32[1,6,64,128]{3,2,1,0:T(8,128)S(1)}, u32[]{:S(2)}, u32[]{:S(2)}) collective-permute-start(f32[1,6,64,128]{3,2,1,0:T(8,128)S(1)} %get-tuple-element.276), channel_id=1, source_target_pairs={{0,8},{8,16},{16,24},{24,0},{1,9},{9,17},{17,25},{25,1},{2,10},{10... | collective-permute-start | bytes 589832 | tf_op jit(solution)/shard_map/ppermute | solution.py:17
  201.3 9.2 %collective-permute-start.9 = (f32[1,6,64,128]{3,2,1,0:T(8,128)S(1)}, f32[1,6,64,128]{3,2,1,0:T(8,128)S(1)}, u32[]{:S(2)}, u32[]{:S(2)}) collective-permute-start(f32[1,6,64,128]{3,2,1,0:T(8,128)S(1)} %get-tuple-element.277), channel_id=1, source_target_pairs={{8,0},{16,8},{24,16},{0,24},{9,1},{17,9},{25,17},{1,25},{10,2},{18... | collective-permute-start | bytes 589832 | tf_op jit(solution)/shard_map/ppermute | solution.py:19
  211.2 8.8 %collective-permute-start.10 = (f32[8,1,64,128]{3,2,1,0:T(8,128)S(1)}, f32[8,1,64,128]{3,2,1,0:T(8,128)S(1)}, u32[]{:S(2)}, u32[]{:S(2)}) collective-permute-start(f32[8,1,64,128]{3,2,1,0:T(8,128)S(1)} %get-tuple-element.268), channel_id=1, source_target_pairs={{0,1},{1,2},{2,3},{3,4},{4,5},{5,6},{6,7},{7,0},{8,9},{9,10},{10,1... | collective-permute-start | bytes 786440 | tf_op jit(solution)/shard_map/ppermute | solution.py:17
  211.3 9.4 %collective-permute-start.11 = (f32[8,1,64,128]{3,2,1,0:T(8,128)S(1)}, f32[8,1,64,128]{3,2,1,0:T(8,128)}, u32[]{:S(2)}, u32[]{:S(2)}) collective-permute-start(f32[8,1,64,128]{3,2,1,0:T(8,128)S(1)} %get-tuple-element.269), channel_id=1, source_target_pairs={{1,0},{2,1},{3,2},{4,3},{5,4},{6,5},{7,6},{0,7},{9,8},{10,9},{11,1... | collective-permute-start | bytes 786440 | tf_op jit(solution)/shard_map/ppermute | solution.py:19
  240.3 4.1 %copy-start = (f32[36,32,128]{2,1,0:T(8,128)S(1)}, f32[36,32,128]{2,1,0:T(8,128)}, u32[]{:S(2)}) copy-start(f32[36,32,128]{2,1,0:T(8,128)} %get-tuple-element.577) | copy-start | bytes 1769476 | tf_op jit(solution)/shard_map/while
  240.3 4.1 %copy-start.2 = (f32[36,32,128]{2,1,0:T(8,128)S(1)}, f32[36,32,128]{2,1,0:T(8,128)}, u32[]{:S(2)}) copy-start(f32[36,32,128]{2,1,0:T(8,128)} %get-tuple-element.578) | copy-start | bytes 1769476 | tf_op jit(solution)/shard_map/while
  247.8 4.1 %copy-start = (f32[36,32,128]{2,1,0:T(8,128)S(1)}, f32[36,32,128]{2,1,0:T(8,128)}, u32[]{:S(2)}) copy-start(f32[36,32,128]{2,1,0:T(8,128)} %get-tuple-element.577) | copy-start | bytes 1769476 | tf_op jit(solution)/shard_map/while
  247.8 4.1 %copy-start.2 = (f32[36,32,128]{2,1,0:T(8,128)S(1)}, f32[36,32,128]{2,1,0:T(8,128)}, u32[]{:S(2)}) copy-start(f32[36,32,128]{2,1,0:T(8,128)} %get-tuple-element.578) | copy-start | bytes 1769476 | tf_op jit(solution)/shard_map/while
  255.3 4.1 %copy-start = (f32[36,32,128]{2,1,0:T(8,128)S(1)}, f32[36,32,128]{2,1,0:T(8,128)}, u32[]{:S(2)}) copy-start(f32[36,32,128]{2,1,0:T(8,128)} %get-tuple-element.577) | copy-start | bytes 1769476 | tf_op jit(solution)/shard_map/while
  255.3 4.1 %copy-start.2 = (f32[36,32,128]{2,1,0:T(8,128)S(1)}, f32[36,32,128]{2,1,0:T(8,128)}, u32[]{:S(2)}) copy-start(f32[36,32,128]{2,1,0:T(8,128)} %get-tuple-element.578) | copy-start | bytes 1769476 | tf_op jit(solution)/shard_map/while
  262.8 4.1 %copy-start = (f32[36,32,128]{2,1,0:T(8,128)S(1)}, f32[36,32,128]{2,1,0:T(8,128)}, u32[]{:S(2)}) copy-start(f32[36,32,128]{2,1,0:T(8,128)} %get-tuple-element.577) | copy-start | bytes 1769476 | tf_op jit(solution)/shard_map/while
  262.8 4.1 %copy-start.2 = (f32[36,32,128]{2,1,0:T(8,128)S(1)}, f32[36,32,128]{2,1,0:T(8,128)}, u32[]{:S(2)}) copy-start(f32[36,32,128]{2,1,0:T(8,128)} %get-tuple-element.578) | copy-start | bytes 1769476 | tf_op jit(solution)/shard_map/while
  270.2 4.1 %copy-start = (f32[36,32,128]{2,1,0:T(8,128)S(1)}, f32[36,32,128]{2,1,0:T(8,128)}, u32[]{:S(2)}) copy-start(f32[36,32,128]{2,1,0:T(8,128)} %get-tuple-element.577) | copy-start | bytes 1769476 | tf_op jit(solution)/shard_map/while
  270.2 4.1 %copy-start.2 = (f32[36,32,128]{2,1,0:T(8,128)S(1)}, f32[36,32,128]{2,1,0:T(8,128)}, u32[]{:S(2)}) copy-start(f32[36,32,128]{2,1,0:T(8,128)} %get-tuple-element.578) | copy-start | bytes 1769476 | tf_op jit(solution)/shard_map/while
  277.7 4.1 %copy-start = (f32[36,32,128]{2,1,0:T(8,128)S(1)}, f32[36,32,128]{2,1,0:T(8,128)}, u32[]{:S(2)}) copy-start(f32[36,32,128]{2,1,0:T(8,128)} %get-tuple-element.577) | copy-start | bytes 1769476 | tf_op jit(solution)/shard_map/while
  277.7 4.1 %copy-start.2 = (f32[36,32,128]{2,1,0:T(8,128)S(1)}, f32[36,32,128]{2,1,0:T(8,128)}, u32[]{:S(2)}) copy-start(f32[36,32,128]{2,1,0:T(8,128)} %get-tuple-element.578) | copy-start | bytes 1769476 | tf_op jit(solution)/shard_map/while
  (72 other events, 85.5 us)
where the time goes:
time: 337 us; the launch traced here: 336 us
  matrix products  108 us (32%)
  local copies, waits for them, and re-layouts  93.3 us (28%)
  blocking collectives  39.2 us (12%)
  waiting for transfers between devices  27.5 us (8%)
  other arithmetic  24.5 us (7%)
  loops' own time  21.9 us (6%)
  starting transfers between devices  20.8 us (6%)
    dot_general x27, matrix products, accumulate(): jnp.einsum('npb,nba->npa', piece, chosen, precision=lax.Precision.HIGHEST)  108 us
    while x216, local copies, waits for them, and re-layouts  44.5 us
    psum x1, blocking collectives, reduce_one(): return lax.psum(intersection(probes, field), ('gx', 'gy')) * scale  39.2 us
    unnamed x36, local copies, waits for them, and re-layouts  22.6 us
    ppermute x6, waiting for transfers between devices, with_halo(): lax.ppermute(tail, axis, [(i, (i + 1) % count) for i in range(count)])  22.5 us
    another operation x3, loops' own time, apply_hamiltonian(): lax.fori_loop(0, slot_bound, accumulate, (zeros, zeros))  21.9 us
    gather x27, local copies, waits for them, and re-layouts, accumulate(): piece = jnp.take(source, flat_partner[:, slot], axis=0)  16.9 us
    ppermute x6, starting transfers between devices, with_halo(): lax.ppermute(head, axis, [((i + 1) % count, i) for i in range(count)])  16 us
  transfers between devices with their start and end apart: 12, of which 8 were waited for; matrix products, arithmetic and copies ran while one was open for 6% of the time, Pallas kernels for 0%

commit v1 on v0

--- a/solution.py
+++ b/solution.py
@@ -5,6 +5,12 @@
 from jax.sharding import PartitionSpec as P
 
 STEPS = 3
+
+
+def summed_here(x, axis):
+    blocks = lax.all_gather(x, axis, axis=0, tiled=False)
+    summed = blocks.sum(axis=0)
+    return summed
 
 
 def with_halo(cells, sides, width):
@@ -84,7 +90,7 @@
     scale = 1.0 / math.sqrt(total_x * total_y * block)
 
     def reduce_one(field):
-        return lax.psum(intersection(probes, field), ("gx", "gy")) * scale
+        return summed_here(intersection(probes, field), ("gx", "gy")) * scale
 
     before = probes
     current = apply_hamiltonian(probes)

time: 337 us -> 412 us (1.22)
  blocking collectives: 39.2 us -> 112 us
    all_gather x0 -> x3, blocking collectives: none -> 112 us  [summed_here(): blocks = lax.all_gather(x, axis, axis=0, tiled=False)]
    psum x1 -> x0, blocking collectives: 39.2 us -> none  [reduce_one(): return lax.psum(intersection(probes, field), ('gx', 'gy')) * scale]
  transfers between devices with their start and end apart: 12 -> 12, of which waited for: 8 -> 8; matrix products, arithmetic and copies ran while one was open for 6% -> 5% of each run, Pallas kernels for 0% -> 0%
where the time goes in v1:
time: 412 us; the launch traced here: 409 us
  blocking collectives  112 us (27%)
  matrix products  108 us (26%)
  local copies, waits for them, and re-layouts  93.8 us (23%)
  waiting for transfers between devices  27.5 us (7%)
  other arithmetic  24.6 us (6%)
  loops' own time  21.2 us (5%)
  starting transfers between devices  20.8 us (5%)
    all_gather x3, blocking collectives, summed_here(): blocks = lax.all_gather(x, axis, axis=0, tiled=False)  112 us
    dot_general x27, matrix products, accumulate(): jnp.einsum('npb,nba->npa', piece, chosen, precision=lax.Precision.HIGHEST)  108 us
    while x216, local copies, waits for them, and re-layouts  45 us
    ppermute x6, waiting for transfers between devices, with_halo(): lax.ppermute(tail, axis, [(i, (i + 1) % count) for i in range(count)])  22.5 us
    unnamed x36, local copies, waits for them, and re-layouts  22.5 us
    another operation x3, loops' own time, apply_hamiltonian(): lax.fori_loop(0, slot_bound, accumulate, (zeros, zeros))  21.2 us
    gather x27, local copies, waits for them, and re-layouts, accumulate(): piece = jnp.take(source, flat_partner[:, slot], axis=0)  16.9 us
    ppermute x6, starting transfers between devices, with_halo(): lax.ppermute(head, axis, [((i + 1) % count, i) for i in range(count)])  16 us
  transfers between devices with their start and end apart: 12, of which 8 were waited for; matrix products, arithmetic and copies ran while one was open for 5% of the time, Pallas kernels for 0%

profile of v1, /device:TPU:0, one launch (start us, length us, event | category | flops | bytes accessed | tf_op | source)
XLA Modules:
  0.0 408.7 jit_solution(12544108775933876293)
XLA Ops:
  0.6 1.1 fusion.46
  1.8 3.0 collective-permute-start
  4.8 1.0 collective-permute-start.1
  5.8 1.3 fusion.47
  7.1 2.8 sine_reduce_fusion
  11.6 3.5 collective-permute-done.1
  15.2 1.2 copy-done.21
  16.4 3.5 collective-permute-start.3
  20.4 15.4 %copy.22 = f32[6,6,9,128,128]{4,3,1,0,2:T(8,128)} copy(f32[6,6,9,128,128]{4,3,2,1,0:T(8,128)} %param.15) | data formatting | bytes 42467328 | tf_op args[1]
  36.5 1.6 pad_maximum_fusion
  38.9 0.9 broadcast.58.clone.4
  39.8 67.5 %while.36 = (s32[]{:T(128)}, f32[36,32,128]{2,1,0:T(8,128)}, f32[36,32,128]{2,1,0:T(8,128)}, s32[]{:T(128)}, f32[36,9]{0,1:T(8,128)S(1)}, /*index=5*/s32[36,9]{0...) while((s32[]{:T(128)}, f32[36,32,128]{2,1,0:T(8,128)}, ...), condition=%wide.region_2.4_spmd, body=%wide.region_1.3_spmd.sunk | while | flops 454460640 | bytes 20059900 | solution.py:87
  41.1 4.0 fusion.62
  48.6 4.0 fusion.62
  56.0 4.0 fusion.62
  63.4 4.0 fusion.62
  70.9 4.0 fusion.62
  78.3 4.0 fusion.62
  85.7 4.0 fusion.62
  93.2 4.0 fusion.62
  100.6 4.0 fusion.62
  107.4 1.2 constant_dynamic-update-slice_fusion.4
  108.7 1.5 collective-permute-start.4
  110.2 1.4 collective-permute-start.5
  111.7 5.0 %collective-permute-done.4 = f32[1,6,64,128]{3,2,1,0:T(8,128)S(1)} collective-permute-done((f32[1,6,64,128]{3,2,1,0:T(8,128)S(1)}, f32[1,6,64,128]{3,2,1,0:T(8,128)S(1)}, u32[]{:S(2)}, u32[]{:S(2)}) %collective-permute-start.4) | collective-permute-done | bytes 196640 | tf_op jit(solution)/shard_map/ppermute | solution.py:23
  116.7 1.0 collective-permute-done.5
  118.5 3.5 collective-permute-start.7
  122.0 5.8 %collective-permute-done.6 = f32[8,1,64,128]{3,2,1,0:T(8,128)S(1)} collective-permute-done((f32[8,1,64,128]{3,2,1,0:T(8,128)S(1)}, f32[8,1,64,128]{3,2,1,0:T(8,128)S(1)}, u32[]{:S(2)}, u32[]{:S(2)}) %collective-permute-start.6) | collective-permute-done | bytes 262176 | tf_op jit(solution)/shard_map/ppermute | solution.py:23
  128.5 1.3 pad_maximum_fusion.1
  129.8 0.9 broadcast.58.clone.1
  130.7 0.9 broadcast.58.clone.2
  131.6 67.8 %while.37 = (s32[]{:T(128)}, f32[36,32,128]{2,1,0:T(8,128)}, f32[36,32,128]{2,1,0:T(8,128)}, s32[]{:T(128)}, f32[36,9]{0,1:T(8,128)S(1)}, /*index=5*/s32[36,9]{0...) while((s32[]{:T(128)}, f32[36,32,128]{2,1,0:T(8,128)}, ...), condition=%wide.region_4.6_spmd, body=%wide.region_3.5_spmd.sunk | while | flops 454460640 | bytes 20059900 | solution.py:87
  133.0 4.0 fusion.66
  140.4 4.0 fusion.66
  147.9 4.0 fusion.66
  155.4 4.0 fusion.66
  162.8 4.0 fusion.66
  170.3 4.0 fusion.66
  177.8 4.0 fusion.66
  185.2 4.0 fusion.66
  192.7 4.0 fusion.66
  199.5 1.4 maximum_multiply_fusion
  201.4 2.9 collective-permute-start.9
  204.3 5.7 %collective-permute-done.8 = f32[1,6,64,128]{3,2,1,0:T(8,128)S(1)} collective-permute-done((f32[1,6,64,128]{3,2,1,0:T(8,128)S(1)}, f32[1,6,64,128]{3,2,1,0:T(8,128)S(1)}, u32[]{:S(2)}, u32[]{:S(2)}) %collective-permute-start.8) | collective-permute-done | bytes 196640 | tf_op jit(solution)/shard_map/ppermute | solution.py:23
  211.4 3.5 collective-permute-start.11
  214.9 5.2 %collective-permute-done.10 = f32[8,1,64,128]{3,2,1,0:T(8,128)S(1)} collective-permute-done((f32[8,1,64,128]{3,2,1,0:T(8,128)S(1)}, f32[8,1,64,128]{3,2,1,0:T(8,128)S(1)}, u32[]{:S(2)}, u32[]{:S(2)}) %collective-permute-start.10) | collective-permute-done | bytes 262176 | tf_op jit(solution)/shard_map/ppermute | solution.py:23
  220.8 1.3 pad_maximum_fusion.2
  222.1 0.9 broadcast.58
  223.9 67.8 %while.38 = (s32[]{:T(128)}, f32[36,32,128]{2,1,0:T(8,128)}, f32[36,32,128]{2,1,0:T(8,128)}, s32[]{:T(128)}, f32[36,9]{0,1:T(8,128)S(1)}, /*index=5*/s32[36,9]{0...) while((s32[]{:T(128)}, f32[36,32,128]{2,1,0:T(8,128)}, ...), condition=%wide.region_6.8_spmd, body=%wide.region_5.7_spmd.sunk | while | flops 454460640 | bytes 20059900 | solution.py:87
  225.4 4.0 fusion.70
  232.9 4.0 fusion.70
  240.3 4.0 fusion.70
  247.8 4.0 fusion.70
  255.2 4.0 fusion.70
  262.7 4.0 fusion.70
  270.1 4.0 fusion.70
  277.6 4.0 fusion.70
  285.0 4.0 fusion.70
  291.8 1.4 maximum_multiply_fusion.1
  293.6 1.1 copy-done.16
  295.0 1.2 add_reduce_fusion.2
  296.3 36.5 %all-gather.3 = f32[32,2,32]{2,1,0:T(2,128)S(1)} all-gather(f32[1,2,32]{2,1,0:T(2,128)S(1)} %maximum_bitcast_fusion), channel_id=2, replica_groups=mesh['gx'=4,'gy'=8] {'gx','gy'}, dimensions={0}, use_global_device_ids=true | all-gather | bytes 8448 | tf_op jit(solution)/shard_map/all_gather | solution.py:11
  332.8 38.4 %all-gather.4 = f32[32,2,32]{2,1,0:T(2,128)S(1)} all-gather(f32[1,2,32]{2,1,0:T(2,128)S(1)} %maximum_bitcast_fusion.1), channel_id=3, replica_groups=mesh['gx'=4,'gy'=8] {'gx','gy'}, dimensions={0}, use_global_device_ids=true | all-gather | bytes 8448 | tf_op jit(solution)/shard_map/all_gather | solution.py:11
  371.3 36.8 %all-gather.5 = f32[32,2,32]{2,1,0:T(2,128)S(1)} all-gather(f32[1,2,32]{2,1,0:T(2,128)S(1)} %maximum_bitcast_fusion.2), channel_id=4, replica_groups=mesh['gx'=4,'gy'=8] {'gx','gy'}, dimensions={0}, use_global_device_ids=true | all-gather | bytes 8448 | tf_op jit(solution)/shard_map/all_gather | solution.py:11
  (424 shorter events, 84.0 us)
Async XLA Ops:
  0.6 10.9 %copy-start.17 = (f32[6,6,64,128]{3,2,1,0:T(8,128)S(1)}, f32[6,6,64,128]{3,2,1,0:T(8,128)}, u32[]{:S(2)}) copy-start(f32[6,6,64,128]{3,2,1,0:T(8,128)} %param.14) | copy-start | bytes 3538948
  1.8 9.7 %collective-permute-start = (f32[1,6,64,128]{3,2,1,0:T(8,128)S(1)}, f32[1,6,64,128]{3,2,1,0:T(8,128)S(1)}, u32[]{:S(2)}, u32[]{:S(2)}) collective-permute-start(f32[1,6,64,128]{3,2,1,0:T(8,128)S(1)} %get-tuple-element.305), channel_id=1, source_target_pairs={{0,8},{8,16},{16,24},{24,0},{1,9},{9,17},{17,25},{25,1},{2,10},{10... | collective-permute-start | bytes 589832 | tf_op jit(solution)/shard_map/ppermute | solution.py:23
  4.8 10.3 %collective-permute-start.1 = (f32[1,6,64,128]{3,2,1,0:T(8,128)S(1)}, f32[1,6,64,128]{3,2,1,0:T(8,128)S(1)}, u32[]{:S(2)}, u32[]{:S(2)}) collective-permute-start(f32[1,6,64,128]{3,2,1,0:T(8,128)S(1)} %get-tuple-element.304), channel_id=1, source_target_pairs={{8,0},{16,8},{24,16},{0,24},{9,1},{17,9},{25,17},{1,25},{10,2},{18... | collective-permute-start | bytes 589832 | tf_op jit(solution)/shard_map/ppermute | solution.py:25
  11.6 8.6 %copy-start.26 = (s32[6,6,9]{2,1,0:T(8,128)S(1)}, s32[6,6,9]{2,1,0:T(8,128)}, u32[]{:S(2)}) copy-start(s32[6,6,9]{2,1,0:T(8,128)} %param.16) | copy-start | bytes 3892
  16.4 20.1 %collective-permute-start.2 = (f32[8,1,64,128]{3,2,1,0:T(8,128)S(1)}, f32[8,1,64,128]{3,2,1,0:T(8,128)S(1)}, u32[]{:S(2)}, u32[]{:S(2)}) collective-permute-start(f32[8,1,64,128]{3,2,1,0:T(8,128)S(1)} %get-tuple-element.296), channel_id=1, source_target_pairs={{0,1},{1,2},{2,3},{3,4},{4,5},{5,6},{6,7},{7,0},{8,9},{9,10},{10,1... | collective-permute-start | bytes 786440 | tf_op jit(solution)/shard_map/ppermute | solution.py:23
  16.4 20.0 %collective-permute-start.3 = (f32[8,1,64,128]{3,2,1,0:T(8,128)S(1)}, f32[8,1,64,128]{3,2,1,0:T(8,128)S(1)}, u32[]{:S(2)}, u32[]{:S(2)}) collective-permute-start(f32[8,1,64,128]{3,2,1,0:T(8,128)S(1)} %get-tuple-element.297), channel_id=1, source_target_pairs={{1,0},{2,1},{3,2},{4,3},{5,4},{6,5},{7,6},{0,7},{9,8},{10,9},{11,1... | collective-permute-start | bytes 786440 | tf_op jit(solution)/shard_map/ppermute | solution.py:25
  20.4 15.4 %copy-start.27 = (s32[6,6]{1,0:T(8,128)S(1)}, s32[6,6]{1,0:T(8,128)}, u32[]{:S(2)}) copy-start(s32[6,6]{1,0:T(8,128)} %param.18) | copy-start | bytes 436
  41.1 4.1 copy-start
  41.1 4.1 copy-start.2
  48.5 4.1 copy-start
  48.6 4.1 copy-start.2
  56.0 4.1 copy-start
  56.0 4.1 copy-start.2
  63.4 4.1 copy-start
  63.4 4.1 copy-start.2
  70.9 4.1 copy-start
  70.9 4.1 copy-start.2
  78.3 4.1 copy-start
  78.3 4.1 copy-start.2
  85.7 4.1 copy-start
  85.7 4.1 copy-start.2
  93.2 4.1 copy-start
  93.2 4.1 copy-start.2
  100.6 4.1 copy-start
  100.6 4.1 copy-start.2
  108.6 19.8 %copy-start.13 = (f32[36,64,128]{2,1,0:T(8,128)}, f32[36,64,128]{2,1,0:T(8,128)S(1)}, u32[]{:S(2)}) copy-start(f32[36,64,128]{2,1,0:T(8,128)S(1)} %constant_dynamic-update-slice_fusion.3) | copy-start | bytes 3538948
  108.7 8.0 %collective-permute-start.4 = (f32[1,6,64,128]{3,2,1,0:T(8,128)S(1)}, f32[1,6,64,128]{3,2,1,0:T(8,128)S(1)}, u32[]{:S(2)}, u32[]{:S(2)}) collective-permute-start(f32[1,6,64,128]{3,2,1,0:T(8,128)S(1)} %get-tuple-element.302), channel_id=1, source_target_pairs={{0,8},{8,16},{16,24},{24,0},{1,9},{9,17},{17,25},{25,1},{2,10},{10... | collective-permute-start | bytes 589832 | tf_op jit(solution)/shard_map/ppermute | solution.py:23
  110.2 7.4 %collective-permute-start.5 = (f32[1,6,64,128]{3,2,1,0:T(8,128)S(1)}, f32[1,6,64,128]{3,2,1,0:T(8,128)S(1)}, u32[]{:S(2)}, u32[]{:S(2)}) collective-permute-start(f32[1,6,64,128]{3,2,1,0:T(8,128)S(1)} %get-tuple-element.303), channel_id=1, source_target_pairs={{8,0},{16,8},{24,16},{0,24},{9,1},{17,9},{25,17},{1,25},{10,2},{18... | collective-permute-start | bytes 589832 | tf_op jit(solution)/shard_map/ppermute | solution.py:25
  118.4 9.4 %collective-permute-start.6 = (f32[8,1,64,128]{3,2,1,0:T(8,128)S(1)}, f32[8,1,64,128]{3,2,1,0:T(8,128)S(1)}, u32[]{:S(2)}, u32[]{:S(2)}) collective-permute-start(f32[8,1,64,128]{3,2,1,0:T(8,128)S(1)} %get-tuple-element.294), channel_id=1, source_target_pairs={{0,1},{1,2},{2,3},{3,4},{4,5},{5,6},{6,7},{7,0},{8,9},{9,10},{10,1... | collective-permute-start | bytes 786440 | tf_op jit(solution)/shard_map/ppermute | solution.py:23
  118.5 10.0 %collective-permute-start.7 = (f32[8,1,64,128]{3,2,1,0:T(8,128)S(1)}, f32[8,1,64,128]{3,2,1,0:T(8,128)}, u32[]{:S(2)}, u32[]{:S(2)}) collective-permute-start(f32[8,1,64,128]{3,2,1,0:T(8,128)S(1)} %get-tuple-element.295), channel_id=1, source_target_pairs={{1,0},{2,1},{3,2},{4,3},{5,4},{6,5},{7,6},{0,7},{9,8},{10,9},{11,1... | collective-permute-start | bytes 786440 | tf_op jit(solution)/shard_map/ppermute | solution.py:25
  132.9 4.1 copy-start.5
  132.9 4.1 copy-start.7
  140.4 4.1 copy-start.5
  140.4 4.1 copy-start.7
  147.9 4.1 copy-start.5
  147.9 4.1 copy-start.7
  155.3 4.1 copy-start.5
  155.3 4.1 copy-start.7
  162.8 4.1 copy-start.5
  162.8 4.1 copy-start.7
  170.3 4.1 copy-start.5
  170.3 4.1 copy-start.7
  177.7 4.1 copy-start.5
  177.7 4.1 copy-start.7
  185.2 4.1 copy-start.5
  185.2 4.1 copy-start.7
  192.7 4.1 copy-start.5
  201.3 19.5 %copy-start.15 = (f32[6,6,64,128]{3,2,1,0:T(8,128)}, f32[6,6,64,128]{3,2,1,0:T(8,128)S(1)}, u32[]{:S(2)}) copy-start(f32[6,6,64,128]{3,2,1,0:T(8,128)S(1)} %sub.47) | copy-start | bytes 3538948
  201.3 8.7 %collective-permute-start.8 = (f32[1,6,64,128]{3,2,1,0:T(8,128)S(1)}, f32[1,6,64,128]{3,2,1,0:T(8,128)S(1)}, u32[]{:S(2)}, u32[]{:S(2)}) collective-permute-start(f32[1,6,64,128]{3,2,1,0:T(8,128)S(1)} %get-tuple-element.300), channel_id=1, source_target_pairs={{0,8},{8,16},{16,24},{24,0},{1,9},{9,17},{17,25},{25,1},{2,10},{10... | collective-permute-start | bytes 589832 | tf_op jit(solution)/shard_map/ppermute | solution.py:23
  201.4 9.2 %collective-permute-start.9 = (f32[1,6,64,128]{3,2,1,0:T(8,128)S(1)}, f32[1,6,64,128]{3,2,1,0:T(8,128)S(1)}, u32[]{:S(2)}, u32[]{:S(2)}) collective-permute-start(f32[1,6,64,128]{3,2,1,0:T(8,128)S(1)} %get-tuple-element.301), channel_id=1, source_target_pairs={{8,0},{16,8},{24,16},{0,24},{9,1},{17,9},{25,17},{1,25},{10,2},{18... | collective-permute-start | bytes 589832 | tf_op jit(solution)/shard_map/ppermute | solution.py:25
  211.3 8.8 %collective-permute-start.10 = (f32[8,1,64,128]{3,2,1,0:T(8,128)S(1)}, f32[8,1,64,128]{3,2,1,0:T(8,128)S(1)}, u32[]{:S(2)}, u32[]{:S(2)}) collective-permute-start(f32[8,1,64,128]{3,2,1,0:T(8,128)S(1)} %get-tuple-element.292), channel_id=1, source_target_pairs={{0,1},{1,2},{2,3},{3,4},{4,5},{5,6},{6,7},{7,0},{8,9},{9,10},{10,1... | collective-permute-start | bytes 786440 | tf_op jit(solution)/shard_map/ppermute | solution.py:23
  211.4 9.4 %collective-permute-start.11 = (f32[8,1,64,128]{3,2,1,0:T(8,128)S(1)}, f32[8,1,64,128]{3,2,1,0:T(8,128)}, u32[]{:S(2)}, u32[]{:S(2)}) collective-permute-start(f32[8,1,64,128]{3,2,1,0:T(8,128)S(1)} %get-tuple-element.293), channel_id=1, source_target_pairs={{1,0},{2,1},{3,2},{4,3},{5,4},{6,5},{7,6},{0,7},{9,8},{10,9},{11,1... | collective-permute-start | bytes 786440 | tf_op jit(solution)/shard_map/ppermute | solution.py:25
  225.4 4.1 copy-start.9
  225.4 4.1 copy-start.11
  240.3 4.1 copy-start.9
  240.3 4.1 copy-start.11
  255.2 4.1 copy-start.9
  255.2 4.1 copy-start.11
  270.1 4.1 copy-start.9
  270.1 4.1 copy-start.11
  277.6 4.1 copy-start.9
  277.6 4.1 copy-start.11
  285.0 4.1 copy-start.9
  285.0 4.1 copy-start.11
  (72 other events, 86.0 us)
